TPU v7x, 32 devices: a whole 2x2x4 slice. The times are simulated.
32 devices in a mesh: grp: 2 (over y), ctx: 4 (over z), head: 2 (over x), sub: 2 (over core).
Axes of the slice: x: 2, y: 2, z: 4, core: 2. Of those that a mesh axis runs over, the one named last changes fastest.
Arguments:
- queries: bfloat16 [512, 16384], P(('grp', 'ctx', 'head', 'sub')), parts along dimension 0, may hold values from -400 to 400
- kv_cache: bfloat16 [2, 8192, 1024], P(None, ('grp', 'ctx', 'sub'), 'head'), parts along dimension 1, may hold values from -6 to 6
- page_counts: int32 [8], P('grp'), parts along dimension 0, may hold values from 1 to 4, as said below
Outputs:
- attended: bfloat16 [512, 16384], P(('grp', 'ctx', 'head', 'sub')), parts along dimension 0
There are 2 independent parts, one for each index of `grp`. A program takes and returns all parts, laid end to end along the dimension named above; each array names one. Nothing has to cross between parts.
Inputs may be any that keep to these rules, and one draw needn't show every extreme that they name: `page_counts`: each count is at least 1, the counts sum to exactly 8, and one request has exactly 4 pages.
All inputs are finite; a program needn't handle non-finite values.
Results may differ from a plain program's by a relative error of at most 0.014.
Values may be sent and summed in bfloat16 or wider, within the bound.
A program may use at most 64 MiB of HBM per device.

v0:
```python
import jax
import jax.numpy as jnp
from jax import lax
from jax.sharding import PartitionSpec as P

HQ = 128
KVH = 8
HD = 128
REQS = 4
QR = 64
PAGE = 256
SPAN = 256


NEG = -1e30


def from_behind(array, axis, by):
    count = lax.axis_size(axis)
    pairs = [(i, i + by) for i in range(count) if 0 <= i + by < count]
    return lax.ppermute(array, axis, pairs)


def per_device(queries, kv_cache, page_counts):
    per_group = HQ // KVH
    local_heads = kv_cache.shape[2] // HD
    ctx_size = lax.axis_size("ctx")
    sub_size = lax.axis_size("sub")
    head_count = lax.axis_size("head")
    tok_rows = queries.shape[0]
    score_scale = HD ** (-0.5)
    regrouped = lax.all_to_all(queries, "head", split_axis=1, concat_axis=0, tiled=True)
    all_queries = lax.all_gather(regrouped, ("ctx", "sub"), axis=0, tiled=True)
    all_queries = all_queries.reshape(SPAN, local_heads, per_group, HD)
    page_ends = jnp.cumsum(page_counts)
    ctx_rows = SPAN // ctx_size
    offsets = jnp.arange(QR, dtype=jnp.int32)
    columns = jnp.arange(PAGE, dtype=jnp.int32)
    flat_index = lax.axis_index("ctx") * sub_size + lax.axis_index("sub")
    pages_here = kv_cache.shape[1] // PAGE
    base_pages = pages_here * ctx_size * sub_size // 2
    initial = (
        jnp.full((SPAN, local_heads, per_group), NEG, jnp.float32),
        jnp.zeros((SPAN, local_heads, per_group), jnp.float32),
        jnp.zeros((SPAN, local_heads, per_group, HD), jnp.float32),
    )
    half_rows = kv_cache.shape[1] // 2
    arrived = from_behind(kv_cache[:, half_rows:], "ctx", -(ctx_size // 2))
    is_lower = lax.axis_index("ctx") < ctx_size // 2
    source_flat = flat_index + ctx_size // 2 * sub_size
    working = jnp.where(is_lower, arrived, kv_cache[:, :half_rows])
    first_page = jnp.where(
        is_lower, source_flat * pages_here + pages_here // 2, flat_index * pages_here
    )
    page_total = working.shape[1] // PAGE

    def add_page(page_turn, running):
        page_index = first_page + page_turn
        relative = page_index - base_pages
        counted = jnp.sum((relative >= page_ends).astype(jnp.int32))
        request = jnp.where(relative < 0, REQS, counted)

        def update(partial_value):
            run_max, run_sum, run_out = partial_value
            request_id = jnp.minimum(request, REQS - 1)
            row_start = request_id * QR
            gathered = row_start + offsets
            within = gathered % ctx_rows
            ctx_block = gathered // ctx_rows
            sub_part = within // (head_count * tok_rows)
            head_part = within // tok_rows % head_count
            tok_part = within % tok_rows
            natural = ctx_block * ctx_rows + (head_part * sub_size + sub_part) * tok_rows + tok_part
            query_pos = (page_ends[request_id] + base_pages) * PAGE - QR + natural - row_start
            key_pos = page_index * PAGE + columns
            visible = key_pos[None, :] <= query_pos[:, None]
            page_keys = working[0].reshape(PAGE, local_heads, HD)
            page_values = working[1].reshape(PAGE, local_heads, HD)
            query_rows = lax.dynamic_slice_in_dim(all_queries, row_start, QR, 0)
            scores = (
                jnp.einsum(
                    "qkgd,pkd->qkgp", query_rows, page_keys, preferred_element_type=jnp.float32
                )
                * score_scale
            )
            scores = jnp.where(visible[:, None, None, :], scores, NEG)
            old_max = lax.dynamic_slice_in_dim(run_max, row_start, QR, 0)
            old_sum = lax.dynamic_slice_in_dim(run_sum, row_start, QR, 0)
            old_out = lax.dynamic_slice_in_dim(run_out, row_start, QR, 0)
            new_max = jnp.maximum(old_max, jnp.max(scores, axis=3))
            factor = jnp.exp(old_max - new_max)
            numerators = jnp.exp(scores - new_max[..., None])
            new_sum = old_sum * factor + jnp.sum(numerators, axis=3)
            product = jnp.einsum(
                "qkgp,pkd->qkgd",
                numerators.astype(jnp.bfloat16),
                page_values,
                preferred_element_type=jnp.float32,
            )
            new_out = old_out * factor[..., None] + product
            return (
                lax.dynamic_update_slice_in_dim(run_max, new_max, row_start, 0),
                lax.dynamic_update_slice_in_dim(run_sum, new_sum, row_start, 0),
                lax.dynamic_update_slice_in_dim(run_out, new_out, row_start, 0),
            )

        def unchanged(partial_value):
            return partial_value

        return lax.cond(request < REQS, update, unchanged, running)

    run_max, run_sum, run_out = lax.fori_loop(0, page_total, add_page, initial)
    share = SPAN // (ctx_size * sub_size)
    global_max = lax.pmax(run_max, ("ctx", "sub"))
    factor = jnp.exp(run_max - global_max)
    sums_here, outs_here = (
        lax.psum_scatter(
            (run_sum * factor).astype(jnp.bfloat16), ("ctx", "sub"), scatter_dimension=0, tiled=True
        ).astype(jnp.float32),
        lax.psum_scatter(
            (run_out * factor[..., None]).astype(jnp.bfloat16),
            ("ctx", "sub"),
            scatter_dimension=0,
            tiled=True,
        ).astype(jnp.float32),
    )
    finished = (outs_here / sums_here[..., None]).astype(jnp.bfloat16)
    finished = finished.reshape(share, local_heads * per_group * HD)
    return lax.all_to_all(finished, "head", split_axis=0, concat_axis=1, tiled=True)


def solution(mesh):
    return jax.shard_map(
        per_device,
        mesh=mesh,
        in_specs=(
            P(("grp", "ctx", "head", "sub"), None),
            P(None, ("grp", "ctx", "sub"), "head"),
            P("grp"),
        ),
        out_specs=P(("grp", "ctx", "head", "sub"), None),
        check_vma=False,
    )
```

profile of v0, /device:TPU:1, one launch (start us, length us, event | category | flops | bytes accessed | tf_op | source)
XLA Modules:
  0.0 257.5 jit_solution(2261504222026062193)
XLA Ops:
  6.5 1.1 copy.56
  7.6 11.4 %all_to_all.38 = bf16[16,2,8192]{2,0,1:T(8,128)(2,1)} all-to-all(bf16[16,2,8192]{2,0,1:T(8,128)(2,1)S(1)} %bitcast.63), channel_id=1, replica_groups=mesh['grp'=2,'ctx'=4,'head'=2,'sub'=2] {'head'}, dimensions={1} | all-to-all | bytes 1048576 | tf_op jit(solution)/shard_map/all_to_all | solution.py:32
  19.1 1.1 slice.13
  20.4 1.3 collective-permute-start
  21.9 0.6 fusion.18
  23.2 3.9 %broadcast_in_dim.30 = f32[256,4,16,128]{3,2,0,1:T(8,128)} broadcast(f32[]{:T(128)} %constant.129.clone.1), dimensions={} | broadcast | bytes 8388612 | tf_op jit(solution)/shard_map/broadcast_in_dim | solution.py:45
  27.2 46.3 %collective-permute-done = bf16[2,256,512]{1,2,0:T(8,128)(2,1)S(1)} collective-permute-done((bf16[2,256,512]{1,2,0:T(8,128)(2,1)S(1)}, bf16[2,256,512]{1,2,0:T(8,128)(2,1)S(1)}, u32[]{:S(2)}, u32[]{:S(2)}) %collective-permute-start) | collective-permute-done | bytes 524320 | tf_op jit(solution)/shard_map/ppermute | solution.py:21
  73.5 10.5 %all-gather.2.cloned.1.call-done = bf16[256,8192]{1,0:T(8,128)(2,1)} async-done(((bf16[32,8192]{1,0:T(8,128)(2,1)}), bf16[256,8192]{1,0:T(8,128)(2,1)}) %all-gather.2.cloned.1.call-update) | async-done | bytes 4194320 | tf_op jit(solution)/shard_map/all_gather | solution.py:33
  84.0 21.3 %conditional.1 = ((f32[256,4,16]{2,0,1:T(8,128)S(1)}, f32[256,4,16]{2,0,1:T(8,128)S(1)}, f32[256,4,16,128]{3,2,0,1:T(8,128)})) conditional(s32[]{:T(128)} %convert_element_type.27, (f32[256,4,16]{2,0,1:T(8,128)S(1)}, f32[256,4,16]{2,0,1:T(8,128)S(1)}, f32[256,4,16,128]{3,2,0,1:T(8,128)}) %tuple.14, (s32[]{:T(128)}, f32[256,4,16]{2,0,1:T(8,128)S(1)}, ...), branch_computations={%region_2.3_spmd, %region_3.6_spmd} | conditional | flops 549745152 | bytes 43667468 | solution.py:110
  84.0 0.7 dynamic_slice.11
  85.4 6.4 %copy.34 = bf16[256,8192]{0,1:T(8,128)(2,1)} copy(bf16[256,8192]{1,0:T(8,128)(2,1)} %get-tuple-element.132) | data formatting | bytes 8388608 | tf_op jit(solution)/shard_map
  91.8 2.3 constant_dynamic-slice_fusion
  94.1 1.9 copy.46
  96.0 1.6 copy.35
  97.6 1.1 slice_select_fusion
  98.7 0.9 bitcast_reduce_fusion
  99.7 1.7 fusion.2
  101.5 3.8 %fusion.5 = f32[256,4,16,128]{3,2,0,1:T(8,128)} fusion(f32[256,4,16,128]{3,2,0,1:T(8,128)} %get-tuple-element.83, s32[]{:T(128)S(6)} %select_n.49, bf16[256,4,128,1]{0,2,3,1:T(8,128)(2,1)S(1)} %bitcast.67, f32[4,64,16,256]{3,2,1,0:T(8,128)S(1)} %get-tuple-element.147, f32[64,4,16]{2,0,1:T(8,128)S(1)} %get-tuple-element.141, ...), kind=kOutput, calls=%fused_computation.8 | convolution fusion | flops 273678336 | bytes 8699908 | tf_op jit(solution)/shard_map/while/body/eval_jaxpr/cond/branch_1_fun/qkgp,pkd->qkgd/dot_general | solution.py:94
  105.3 0.8 copy-done
  106.2 52.1 %all-reduce.2.cloned.1.call-done = f32[256,4,16]{2,0,1:T(8,128)} async-done(((f32[256,4,16]{2,0,1:T(8,128)}), f32[256,4,16]{2,0,1:T(8,128)}) %all-reduce.2.cloned.1.call-update) | async-done | bytes 65552 | tf_op jit(solution)/shard_map/pmax | solution.py:114
  158.3 2.0 multiply_convert_fusion.1
  160.5 5.2 %multiply_convert_fusion = bf16[256,4,16,128]{3,2,0,1:T(8,128)(2,1)S(1)} fusion(f32[256,4,16,128]{3,2,0,1:T(8,128)} %get-tuple-element.87, f32[256,4,16]{2,0,1:T(8,128)S(1)} %get-tuple-element.143), kind=kLoop, calls=%fused_computation.44 | loop fusion | flops 4194304 | bytes 12648448 | tf_op jit(solution)/shard_map/convert_element_type | solution.py:121
  165.7 1.3 copy.44
  167.1 10.1 %copy.55 = bf16[32,8,64,128]{3,1,2,0:T(8,128)(2,1)} copy(bf16[32,8,64,128]{3,2,1,0:T(8,128)(2,1)S(1)} %bitcast.58) | data formatting | bytes 8388608
  177.2 11.6 %reduce-scatter.6.cloned.1.call-done = bf16[32,4,16]{2,0,1:T(8,128)(2,1)} async-done(((bf16[256,4,16]{2,0,1:T(8,128)(2,1)}), bf16[32,4,16]{2,0,1:T(8,128)(2,1)}) %reduce-scatter.6.cloned.1.call-update) | async-done | bytes 4112 | tf_op jit(solution)/shard_map/reduce_scatter | solution.py:117
  188.8 0.8 convert_element_type.31
  189.6 50.9 %reduce-scatter.8.cloned.1.call-done = bf16[32,8192]{1,0:T(8,128)(2,1)} async-done(((bf16[256,8192]{1,0:T(8,128)(2,1)}), bf16[32,8192]{1,0:T(8,128)(2,1)}) %reduce-scatter.8.cloned.1.call-update) | async-done | bytes 524304
  240.5 1.2 copy.51
  241.7 0.3 divide_convert_fusion
  242.1 0.2 all_to_all.32
  242.3 7.8 %all_to_all.39 = bf16[2,16,8192]{2,1,0:T(8,128)(2,1)S(1)} all-to-all(bf16[2,16,8192]{2,1,0:T(8,128)(2,1)S(1)} %all_to_all.32), channel_id=1, replica_groups=mesh['grp'=2,'ctx'=4,'head'=2,'sub'=2] {'head'}, dimensions={0} | all-to-all | bytes 1048576 | tf_op jit(solution)/shard_map/all_to_all | solution.py:129
  250.2 0.8 copy.49
  (30 shorter events, 1.2 us)
Async XLA Ops:
  6.5 15.2 %copy-start.3 = (s32[4]{0:T(128)S(1)}, s32[4]{0:T(128)}, u32[]{:S(2)}) copy-start(s32[4]{0:T(128)} %param.7) | copy-start | bytes 52
  6.5 77.4 %all-gather.2.cloned.1.call-start = ((), (), s32[]{:S(2)}) async-start(), calls=%async_computation.4 | async-start | bytes 4718592 | tf_op jit(solution)/shard_map/all_gather | solution.py:33
  19.0 139.2 %all-reduce.2.cloned.1.call-start = ((), (), s32[]{:S(2)}) async-start(), calls=%async_computation.5 | async-start | bytes 1048576 | tf_op jit(solution)/shard_map/pmax | solution.py:114
  20.4 53.1 %collective-permute-start = (bf16[2,256,512]{1,2,0:T(8,128)(2,1)S(1)}, bf16[2,256,512]{1,2,0:T(8,128)(2,1)S(1)}, u32[]{:S(2)}, u32[]{:S(2)}) collective-permute-start(bf16[2,256,512]{1,2,0:T(8,128)(2,1)S(1)} %copy.47), channel_id=1, source_target_pairs={{8,0},{12,4},{9,1},{13,5},{10,2},{14,6},{11,3},{15,7},{24,16},{28,... | collective-permute-start | bytes 1572872 | tf_op jit(solution)/shard_map/ppermute | solution.py:21
  84.0 7.8 %copy-start.2 = (bf16[2,256,512]{1,2,0:T(8,128)(2,1)}, bf16[2,256,512]{1,2,0:T(8,128)(2,1)S(1)}, u32[]{:S(2)}) copy-start(bf16[2,256,512]{1,2,0:T(8,128)(2,1)S(1)} %get-tuple-element.80) | copy-start | bytes 1572868 | tf_op jit(solution)/shard_map/while/body/eval_jaxpr/cond
  96.0 2.7 %copy-start.1 = (bf16[64,4,16,128]{3,2,0,1:T(8,128)(2,1)S(1)}, bf16[64,4,16,128]{3,2,0,1:T(8,128)(2,1)}, u32[]{:S(2)}) copy-start(bf16[64,4,16,128]{3,2,0,1:T(8,128)(2,1)} %copy.46) | copy-start | bytes 3145732 | tf_op jit(solution)/shard_map/while/body/eval_jaxpr/cond
  105.3 0.8 copy-start
  106.1 82.7 %reduce-scatter.6.cloned.1.call-start = ((), (), s32[]{:S(2)}) async-start(), calls=%async_computation.6 | async-start | bytes 294912 | tf_op jit(solution)/shard_map/reduce_scatter | solution.py:117
  160.3 80.2 %reduce-scatter.8.cloned.1.call-start = ((), (), s32[]{:S(2)}) async-start(), calls=%async_computation.7 | async-start | bytes 4718592
Sparse Core Ops, SparseCore 0:
  19.1 64.7 all-gather.1
  106.2 51.9 all-reduce.1
  160.5 28.2 reduce-scatter.5
  191.0 49.5 reduce-scatter.7
where the time goes:
time: 262 us; the launch traced here: 258 us
  waiting for transfers between devices  171 us (65%)
  local copies, waits for them, and re-layouts  33.8 us (13%)
  blocking collectives  19.2 us (7%)
  between operations  13.9 us (5%)
  other arithmetic  12.2 us (5%)
  matrix products  4.68 us (2%)
    pmax x1, waiting for transfers between devices, per_device(): global_max = lax.pmax(run_max, ('ctx', 'sub'))  52.1 us
    unnamed x5, waiting for transfers between devices  51 us
    ppermute x1, waiting for transfers between devices, from_behind(): return lax.ppermute(array, axis, pairs)  46.3 us
    unnamed x8, local copies, waits for them, and re-layouts  13.6 us
    reduce_scatter x1, waiting for transfers between devices, per_device(): lax.psum_scatter((run_sum * factor).astype(jnp.bfloat16), ('ctx', 'sub'),...  11.6 us
    all_to_all x1, blocking collectives, per_device(): lax.all_to_all(queries, 'head', split_axis=1, concat_axis=0, tiled=True)  11.4 us
    all_gather x1, waiting for transfers between devices, per_device(): all_queries = lax.all_gather(regrouped, ('ctx', 'sub'), axis=0, tiled=True)  10.5 us
    another operation x2, local copies, waits for them, and re-layouts  7.96 us
  transfers between devices with their start and end apart: 5, of which 5 were waited for; matrix products, arithmetic and copies ran while one was open for 9% of the time, Pallas kernels for 0%

commit v1 on v0

--- a/solution.py
+++ b/solution.py
@@ -1,6 +1,11 @@
+import functools
+import math
+
 import jax
 import jax.numpy as jnp
 from jax import lax
+from jax.experimental import pallas as pl
+from jax.experimental.pallas import tpu as pltpu
 from jax.sharding import PartitionSpec as P
 
 HQ = 128
@@ -13,6 +18,8 @@
 
 
 NEG = -1e30
+MESH = pl.DeviceIdType.MESH
+ROW_BLOCK = 256
 
 
 def from_behind(array, axis, by):
@@ -129,9 +136,378 @@
     return lax.all_to_all(finished, "head", split_axis=0, concat_axis=1, tiled=True)
 
 
+def page_plan(ctx_size, sub_size, pages_here):
+    live = pages_here * ctx_size * sub_size // 2
+    base = live
+    last = ctx_size - 1
+    low = [0 if r == 0 else live // 2 if r == last else r for r in range(ctx_size)]
+    high = [live // 2 if r == 0 else live if r == last else live - (last - r) for r in range(ctx_size)]
+    plane_of = [(base + p) // (pages_here * sub_size) for p in range(live)]
+    core_of = [(base + p) // pages_here % sub_size for p in range(live)]
+    return live, low, high, plane_of, core_of
+
+
+def can_ship(mesh, rows):
+    ctx_size, sub_size, head_size = mesh.shape["ctx"], mesh.shape["sub"], mesh.shape["head"]
+    if ctx_size != REQS or SPAN // ctx_size != QR:
+        return False
+    pages_here = rows // (mesh.shape["grp"] * ctx_size * sub_size) // PAGE
+    if pages_here < 1 or KVH % (head_size * sub_size):
+        return False
+    live, low, high, plane_of, _ = page_plan(ctx_size, sub_size, pages_here)
+    ahead = any(
+        low[r] <= p < high[r] and r > plane_of[p] for r in range(ctx_size) for p in range(live)
+    )
+    return not ahead
+
+
+def ship_kernel(
+    sizes,
+    counts_ref,
+    q_hbm,
+    kv_hbm,
+    out_hbm,
+    kvbuf,
+    qbuf,
+    qs,
+    sbuf,
+    mx,
+    lsum,
+    acc,
+    obuf,
+    q_send,
+    q_recv,
+    o_send,
+    o_recv,
+    kv_send,
+    kv_recv,
+    relay_send,
+):
+    ctx_size, sub_size, head_size, pages_here, local_heads = sizes
+    live, low, high, plane_of, core_of = page_plan(ctx_size, sub_size, pages_here)
+    per_core = local_heads // sub_size
+    group = HQ // KVH
+    width = group * HD
+    plane_devices = head_size * sub_size
+    tok_rows = QR // plane_devices
+    z, x, s = lax.axis_index("ctx"), lax.axis_index("head"), lax.axis_index("sub")
+    mine = x * sub_size + s
+    rows = QR * group
+
+    def pick(values):
+        got = jnp.int32(values[0])
+        for i in range(1, ctx_size):
+            got = jnp.where(z == i, jnp.int32(values[i]), got)
+        return got
+
+    def here(r, p):
+        return low[r] <= p < high[r]
+
+    barrier = pltpu.get_barrier_semaphore()
+    for step in range(1, plane_devices):
+        other = lax.rem(mine + step, plane_devices)
+        pl.semaphore_signal(
+            barrier,
+            device_id={"head": other // sub_size, "sub": other % sub_size},
+            device_id_type=MESH,
+        )
+    for core in range(sub_size):
+        @pl.when(z > 0)
+        def _():
+            pl.semaphore_signal(
+                barrier, device_id={"ctx": z - 1, "sub": core}, device_id_type=MESH
+            )
+
+        @pl.when(z < ctx_size - 1)
+        def _():
+            pl.semaphore_signal(
+                barrier, device_id={"ctx": z + 1, "sub": core}, device_id_type=MESH
+            )
+    amounts = [
+        plane_devices - 1 + (sub_size if r > 0 else 0) + (sub_size if r < ctx_size - 1 else 0)
+        for r in range(ctx_size)
+    ]
+    pl.semaphore_wait(barrier, pick(amounts))
+
+    def q_cols(device, h):
+        return pl.ds(pl.multiple_of((device * per_core + h) * width, width), width)
+
+    def q_copy(h, step):
+        other = lax.rem(mine + step, plane_devices)
+        return pltpu.make_async_remote_copy(
+            src_ref=q_hbm.at[:, q_cols(other, h)],
+            dst_ref=qbuf.at[h, mine],
+            send_sem=q_send.at[h, step],
+            recv_sem=q_recv.at[h, mine],
+            device_id={"head": other // sub_size, "sub": other % sub_size},
+            device_id_type=MESH,
+        )
+
+    def q_own(h):
+        return pltpu.make_async_copy(
+            q_hbm.at[:, q_cols(mine, h)], qbuf.at[h, mine], q_recv.at[h, mine]
+        )
+
+    def o_copy(h, step):
+        other = lax.rem(mine + step, plane_devices)
+        return pltpu.make_async_remote_copy(
+            src_ref=obuf.at[h, other],
+            dst_ref=out_hbm.at[:, q_cols(mine, h)],
+            send_sem=o_send.at[h, step],
+            recv_sem=o_recv.at[h, mine],
+            device_id={"head": other // sub_size, "sub": other % sub_size},
+            device_id_type=MESH,
+        )
+
+    def o_own(h):
+        return pltpu.make_async_copy(
+            obuf.at[h, mine], out_hbm.at[:, q_cols(mine, h)], o_recv.at[h, mine]
+        )
+
+    def kv_source(h, k, p, core):
+        row = p % pages_here * PAGE
+        col = (core * per_core + h) * HD
+        return kv_hbm.at[k, pl.ds(row, PAGE), pl.ds(pl.multiple_of(col, HD), HD)]
+
+    def kv_remote(h, k, p, slot, core, target):
+        return pltpu.make_async_remote_copy(
+            src_ref=kv_source(h, k, p, core),
+            dst_ref=kvbuf.at[h, k, p],
+            send_sem=kv_send.at[h, k, slot, p],
+            recv_sem=kv_recv.at[h, k, p],
+            device_id=target,
+            device_id_type=MESH,
+        )
+
+    def kv_own(h, k, p):
+        return pltpu.make_async_copy(
+            kv_source(h, k, p, s), kvbuf.at[h, k, p], kv_recv.at[h, k, p]
+        )
+
+    def each_source(h, k, remote_act, own_act):
+        for p in range(live):
+            @pl.when((z == plane_of[p]) & (s == core_of[p]))
+            def _():
+                if plane_of[p] > 0 and any(here(r, p) for r in range(plane_of[p])):
+                    for core in range(sub_size):
+                        remote_act(
+                            kv_remote(h, k, p, core, core, {"ctx": z - 1, "sub": core})
+                        )
+                if here(plane_of[p], p):
+                    for step in range(1, sub_size):
+                        other = lax.rem(s + step, sub_size)
+                        remote_act(
+                            kv_remote(h, k, p, sub_size - 1 + step, other, {"sub": other})
+                        )
+                    if own_act is not None:
+                        own_act(kv_own(h, k, p))
+
+    def relay(h, k, p):
+        return pltpu.make_async_remote_copy(
+            src_ref=kvbuf.at[h, k, p],
+            dst_ref=kvbuf.at[h, k, p],
+            send_sem=relay_send.at[h, k, p],
+            recv_sem=kv_recv.at[h, k, p],
+            device_id={"ctx": z - 1},
+            device_id_type=MESH,
+        )
+
+    takes = [
+        [
+            p
+            for p in range(live)
+            if (plane_of[p] > r and any(here(i, p) for i in range(r + 1))) or here(r, p)
+        ]
+        for r in range(ctx_size)
+    ]
+    passes = [
+        [p for p in range(live) if plane_of[p] > r and any(here(i, p) for i in range(r))]
+        for r in range(ctx_size)
+    ]
+    take_low, take_high = pick([t[0] for t in takes]), pick([t[-1] + 1 for t in takes])
+    pass_low = pick([t[0] if t else 0 for t in passes])
+    pass_high = pick([t[-1] + 1 if t else 0 for t in passes])
+    own_low, own_high = pick(low), pick(high)
+
+    first = jnp.int32(0)
+    for r in range(REQS):
+        first = first + jnp.where(z > r, counts_ref[r], 0)
+    count = jnp.int32(0)
+    for r in range(REQS):
+        count = count + jnp.where(z == r, counts_ref[r], 0)
+    first_pos = first * PAGE
+    query_base = (first + count) * PAGE - QR
+    token = lax.broadcasted_iota(jnp.int32, (QR, PAGE), 0)
+    column = lax.broadcasted_iota(jnp.int32, (QR, PAGE), 1)
+    factor = HD ** (-0.5) * math.log2(math.e)
+    block = ROW_BLOCK
+    heads_in_block = block // QR
+
+    def start(copy):
+        copy.start()
+
+    order = [(h, k) for h in range(per_core) for k in range(2)]
+    each_source(0, 0, start, start)
+    for h in range(per_core):
+        for step in range(1, plane_devices):
+            q_copy(h, step).start()
+        q_own(h).start()
+
+    for turn, (h, k) in enumerate(order):
+        if k == 0:
+            for device in range(plane_devices):
+                pltpu.make_async_copy(
+                    q_hbm.at[:, q_cols(0, h)], qbuf.at[h, device], q_recv.at[h, device]
+                ).wait()
+            for j in range(group):
+                for device in range(plane_devices):
+                    qs[pl.ds(j * QR + device * tok_rows, tok_rows), :] = qbuf[
+                        h, device, :, j * HD : (j + 1) * HD
+                    ]
+            mx[...] = jnp.full_like(mx, NEG)
+        else:
+            for b in range(rows // block):
+                sl = pl.ds(b * block, block)
+                mx[sl, :] = jnp.broadcast_to(
+                    jnp.max(mx[sl, :], axis=1, keepdims=True), (block, HD)
+                )
+            lsum[...] = jnp.zeros_like(lsum)
+            acc[...] = jnp.zeros_like(acc)
+
+        def turn_page(p, carry, h=h, k=k):
+            pltpu.make_async_copy(
+                kv_source(h, k, 0, 0), kvbuf.at[h, k, p], kv_recv.at[h, k, p]
+            ).wait()
+
+            @pl.when((p >= pass_low) & (p < pass_high))
+            def _():
+                relay(h, k, p).start()
+
+            @pl.when((p >= own_low) & (p < own_high))
+            def _():
+                field = kvbuf[h, k, p]
+                slot = p - own_low
+                if k == 0:
+                    pos = p * PAGE + column
+                    seen = (pos >= first_pos) & (pos <= query_base + token)
+                    bias = jnp.where(seen, 0.0, NEG)
+                    for b in range(rows // block):
+                        sl = pl.ds(b * block, block)
+                        scores = lax.dot_general(
+                            qs[sl, :],
+                            field,
+                            (((1,), (1,)), ((), ())),
+                            preferred_element_type=jnp.float32,
+                        )
+                        scores = scores.reshape(heads_in_block, QR, PAGE) + bias[None]
+                        scores = scores.reshape(block, PAGE)
+                        sbuf[slot, sl, :] = scores
+                        top = mx[sl, :]
+                        for c in range(PAGE // HD):
+                            top = jnp.maximum(top, scores[:, c * HD : (c + 1) * HD])
+                        mx[sl, :] = top
+                else:
+                    for b in range(rows // block):
+                        sl = pl.ds(b * block, block)
+                        top = mx[sl, :]
+                        parts = [
+                            jnp.exp2((sbuf[slot, sl, c * HD : (c + 1) * HD] - top) * factor)
+                            for c in range(PAGE // HD)
+                        ]
+                        total = lsum[sl, :]
+                        for part in parts:
+                            total = total + part
+                        lsum[sl, :] = total
+                        weights = jnp.concatenate(
+                            [part.astype(jnp.bfloat16) for part in parts], axis=1
+                        )
+                        acc[sl, :] += jnp.dot(
+                            weights, field, preferred_element_type=jnp.float32
+                        )
+
+            return carry
+
+        lax.fori_loop(take_low, take_high, turn_page, 0)
+        if turn + 1 < len(order):
+            each_source(*order[turn + 1], start, start)
+        if k == 1:
+            for j in range(group):
+                sl = pl.ds(j * QR, QR)
+                done = acc[sl, :] / jnp.sum(lsum[sl, :], axis=1, keepdims=True)
+                done = done.astype(jnp.bfloat16)
+                for device in range(plane_devices):
+                    obuf[h, device, :, j * HD : (j + 1) * HD] = done[
+                        device * tok_rows : (device + 1) * tok_rows, :
+                    ]
+            for step in range(1, plane_devices):
+                o_copy(h, step).start()
+            o_own(h).start()
+
+    for h in range(per_core):
+        for device in range(plane_devices):
+            pltpu.make_async_copy(
+                obuf.at[h, device], out_hbm.at[:, q_cols(0, h)], o_recv.at[h, device]
+            ).wait()
+        for step in range(1, plane_devices):
+            q_copy(h, step).wait_send()
+            o_copy(h, step).wait_send()
+        for k in range(2):
+            each_source(h, k, lambda copy: copy.wait_send(), None)
+
+            def drain(p, carry, h=h, k=k):
+                relay(h, k, p).wait_send()
+                return carry
+
+            lax.fori_loop(pass_low, pass_high, drain, 0)
+
+
+def shipped(queries, kv_cache, page_counts):
+    ctx_size, sub_size = lax.axis_size("ctx"), lax.axis_size("sub")
+    head_size = lax.axis_size("head")
+    local_heads = kv_cache.shape[2] // HD
+    pages_here = kv_cache.shape[1] // PAGE
+    per_core = local_heads // sub_size
+    group = HQ // KVH
+    live, low, high, _, _ = page_plan(ctx_size, sub_size, pages_here)
+    slots = max(b - a for a, b in zip(low, high))
+    plane_devices = head_size * sub_size
+    tok_rows = queries.shape[0]
+    rows = QR * group
+    dma = pltpu.SemaphoreType.DMA
+    return pl.pallas_call(
+        functools.partial(ship_kernel, (ctx_size, sub_size, head_size, pages_here, local_heads)),
+        out_shape=jax.ShapeDtypeStruct(queries.shape, jnp.bfloat16),
+        in_specs=[
+            pl.BlockSpec(memory_space=pltpu.SMEM),
+            pl.BlockSpec(memory_space=pl.ANY),
+            pl.BlockSpec(memory_space=pl.ANY),
+        ],
+        out_specs=pl.BlockSpec(memory_space=pl.ANY),
+        scratch_shapes=[
+            pltpu.VMEM((per_core, 2, live, PAGE, HD), jnp.bfloat16),
+            pltpu.VMEM((per_core, plane_devices, tok_rows, group * HD), jnp.bfloat16),
+            pltpu.VMEM((rows, HD), jnp.bfloat16),
+            pltpu.VMEM((slots, rows, PAGE), jnp.float32),
+            pltpu.VMEM((rows, HD), jnp.float32),
+            pltpu.VMEM((rows, HD), jnp.float32),
+            pltpu.VMEM((rows, HD), jnp.float32),
+            pltpu.VMEM((per_core, plane_devices, tok_rows, group * HD), jnp.bfloat16),
+            dma((per_core, plane_devices)),
+            dma((per_core, plane_devices)),
+            dma((per_core, plane_devices)),
+            dma((per_core, plane_devices)),
+            dma((per_core, 2, 2 * sub_size - 1, live)),
+            dma((per_core, 2, live)),
+            dma((per_core, 2, live)),
+        ],
+        compiler_params=pltpu.CompilerParams(
+            collective_id=0, has_side_effects=True, vmem_limit_bytes=40 * 1024 * 1024
+        ),
+    )(page_counts, queries, kv_cache)
+
+
 def solution(mesh):
-    return jax.shard_map(
-        per_device,
+    specs = dict(
         mesh=mesh,
         in_specs=(
             P(("grp", "ctx", "head", "sub"), None),
@@ -141,3 +517,9 @@
         out_specs=P(("grp", "ctx", "head", "sub"), None),
         check_vma=False,
     )
+
+    def run(queries, kv_cache, page_counts):
+        body = shipped if can_ship(mesh, kv_cache.shape[1]) else per_device
+        return jax.shard_map(body, **specs)(queries, kv_cache, page_counts)
+
+    return run

time: 262 us -> 53.6 us (0.20); the launches traced: 258 us -> 53.4 us
  waiting for transfers between devices: 171 us -> 0 us
  Pallas kernels: 0 us -> 49.6 us
  local copies, waits for them, and re-layouts: 33.8 us -> 3.72 us
  blocking collectives: 19.2 us -> 0 us
  between operations: 13.9 us -> 0.01 us
  other arithmetic: 12.2 us -> 0 us
  matrix products: 4.68 us -> 0 us
    pmax x1 -> x0, waiting for transfers between devices: 52.1 us -> none  [per_device(): global_max = lax.pmax(run_max, ('ctx', 'sub'))]
    unnamed x5 -> x0, waiting for transfers between devices: 51 us -> none
    pallas_call x0 -> x1, Pallas kernels: none -> 49.6 us  [shipped(): pl.pallas_call(functools.partial(ship_kernel, (ctx_size, sub_size, head_s...]
    ppermute x1 -> x0, waiting for transfers between devices: 46.3 us -> none  [from_behind(): return lax.ppermute(array, axis, pairs)]
    all_to_all x2 -> x0, blocking collectives: 19.2 us -> none  [the longest x1 11.4 us: per_device(): lax.all_to_all(queries, 'head', split_axis=1, concat_axis=0, tiled=True)]
    reduce_scatter x1 -> x0, waiting for transfers between devices: 11.6 us -> none  [per_device(): lax.psum_scatter((run_sum * factor).astype(jnp.bfloat16), ('ctx', 'sub'),...]
    all_gather x1 -> x0, waiting for transfers between devices: 10.5 us -> none  [per_device(): all_queries = lax.all_gather(regrouped, ('ctx', 'sub'), axis=0, tiled=True)]
    unnamed x8 -> x7, local copies, waits for them, and re-layouts: 13.6 us -> 3.72 us
  transfers between devices with their start and end apart: 5 -> 0, of which waited for: 5 -> 0; matrix products, arithmetic and copies ran while one was open for 9% -> 0% of each run, Pallas kernels for 0% -> 0%
where the time goes in v1:
time: 53.6 us; the launch traced here: 53.4 us
  Pallas kernels  49.6 us (93%)
  local copies, waits for them, and re-layouts  3.72 us (7%)
    pallas_call x1, Pallas kernels, shipped(): pl.pallas_call(functools.partial(ship_kernel, (ctx_size, sub_size, head_s...  49.6 us
    unnamed x7, local copies, waits for them, and re-layouts  3.72 us

profile of v1, /device:TPU:1, one launch (start us, length us, event | category | flops | bytes accessed | tf_op | source)
XLA Modules:
  0.0 53.4 jit_solution(11480840731151183308)
XLA Ops:
  0.0 0.0 copy-start
  0.0 1.2 %copy-done = bf16[2,512,512]{2,1,0:T(8,128)(2,1)S(1)} copy-done((bf16[2,512,512]{2,1,0:T(8,128)(2,1)S(1)}, bf16[2,512,512]{2,1,0:T(8,128)(2,1)}, u32[]{:S(2)}) %copy-start) | copy-done | bytes 1048600
  1.2 0.0 copy-start.1
  1.2 1.0 %copy-done.1 = bf16[16,16384]{1,0:T(8,128)(2,1)S(1)} copy-done((bf16[16,16384]{1,0:T(8,128)(2,1)S(1)}, bf16[16,16384]{1,0:T(8,128)(2,1)}, u32[]{:S(2)}) %copy-start.1) | copy-done | bytes 524312
  2.3 0.0 copy-start.2
  2.3 0.7 %copy-done.2 = s32[4]{0:T(128)S(1)} copy-done((s32[4]{0:T(128)S(1)}, s32[4]{0:T(128)}, u32[]{:S(2)}) %copy-start.2) | copy-done | bytes 40
  2.9 49.6 %shard_map.37 = bf16[16,16384]{1,0:T(8,128)(2,1)S(1)} custom-call(s32[4]{0:T(128)S(1)} %copy-done.2, bf16[16,16384]{1,0:T(8,128)(2,1)S(1)} %copy-done.1, bf16[2,512,512]{2,1,0:T(8,128)(2,1)S(1)} %copy-done), custom_call_target="tpu_custom_call" | custom-call | tf_op jit(solution)/shard_map/pallas_call | solution.py:477
  52.6 0.8 %copy.5 = bf16[16,16384]{1,0:T(8,128)(2,1)} copy(bf16[16,16384]{1,0:T(8,128)(2,1)S(1)} %shard_map.37) | data formatting | bytes 1048576
Async XLA Ops:
  0.0 1.2 %copy-start = (bf16[2,512,512]{2,1,0:T(8,128)(2,1)S(1)}, bf16[2,512,512]{2,1,0:T(8,128)(2,1)}, u32[]{:S(2)}) copy-start(bf16[2,512,512]{2,1,0:T(8,128)(2,1)} %kv_hbm.1) | copy-start | bytes 3145732
  1.2 1.0 %copy-start.1 = (bf16[16,16384]{1,0:T(8,128)(2,1)S(1)}, bf16[16,16384]{1,0:T(8,128)(2,1)}, u32[]{:S(2)}) copy-start(bf16[16,16384]{1,0:T(8,128)(2,1)} %q_hbm.1) | copy-start | bytes 1572868
  2.3 0.7 %copy-start.2 = (s32[4]{0:T(128)S(1)}, s32[4]{0:T(128)}, u32[]{:S(2)}) copy-start(s32[4]{0:T(128)} %counts_ref.1) | copy-start | bytes 52

commit v2 on v1

--- a/solution.py
+++ b/solution.py
@@ -185,7 +185,9 @@
 ):
     ctx_size, sub_size, head_size, pages_here, local_heads = sizes
     live, low, high, plane_of, core_of = page_plan(ctx_size, sub_size, pages_here)
+    hub = plane_of[0]
     per_core = local_heads // sub_size
+    moved = per_core - per_core // 2
     group = HQ // KVH
     width = group * HD
     plane_devices = head_size * sub_size
@@ -203,30 +205,44 @@
     def here(r, p):
         return low[r] <= p < high[r]
 
+    def unit_of(h, r):
+        return h if h < moved else moved + (h - moved) * (hub + 1) + r
+
+    def whole_plane(a, b):
+        return per_core > moved and ((a < hub and b == hub) or (b < hub and a == hub))
+
+    def at(device, plane=None):
+        place = {"head": device // sub_size, "sub": device % sub_size}
+        if plane is not None:
+            place["ctx"] = plane
+        return place
+
     barrier = pltpu.get_barrier_semaphore()
     for step in range(1, plane_devices):
         other = lax.rem(mine + step, plane_devices)
-        pl.semaphore_signal(
-            barrier,
-            device_id={"head": other // sub_size, "sub": other % sub_size},
-            device_id_type=MESH,
-        )
-    for core in range(sub_size):
-        @pl.when(z > 0)
-        def _():
-            pl.semaphore_signal(
-                barrier, device_id={"ctx": z - 1, "sub": core}, device_id_type=MESH
-            )
-
-        @pl.when(z < ctx_size - 1)
-        def _():
-            pl.semaphore_signal(
-                barrier, device_id={"ctx": z + 1, "sub": core}, device_id_type=MESH
-            )
-    amounts = [
-        plane_devices - 1 + (sub_size if r > 0 else 0) + (sub_size if r < ctx_size - 1 else 0)
-        for r in range(ctx_size)
-    ]
+        pl.semaphore_signal(barrier, device_id=at(other), device_id_type=MESH)
+    amounts = []
+    for a in range(ctx_size):
+        amount = plane_devices - 1
+        for b in range(ctx_size):
+            if a == b or not (whole_plane(a, b) or abs(a - b) == 1):
+                continue
+            amount += plane_devices if whole_plane(a, b) else sub_size
+
+            @pl.when(z == a)
+            def _():
+                if whole_plane(a, b):
+                    for device in range(plane_devices):
+                        pl.semaphore_signal(
+                            barrier, device_id=at(device, b), device_id_type=MESH
+                        )
+                else:
+                    for core in range(sub_size):
+                        pl.semaphore_signal(
+                            barrier, device_id={"ctx": b, "sub": core}, device_id_type=MESH
+                        )
+
+        amounts.append(amount)
     pl.semaphore_wait(barrier, pick(amounts))
 
     def q_cols(device, h):
@@ -236,32 +252,57 @@
         other = lax.rem(mine + step, plane_devices)
         return pltpu.make_async_remote_copy(
             src_ref=q_hbm.at[:, q_cols(other, h)],
-            dst_ref=qbuf.at[h, mine],
+            dst_ref=qbuf.at[unit_of(h, hub), mine],
             send_sem=q_send.at[h, step],
-            recv_sem=q_recv.at[h, mine],
-            device_id={"head": other // sub_size, "sub": other % sub_size},
+            recv_sem=q_recv.at[unit_of(h, hub), mine],
+            device_id=at(other),
             device_id_type=MESH,
         )
 
     def q_own(h):
         return pltpu.make_async_copy(
-            q_hbm.at[:, q_cols(mine, h)], qbuf.at[h, mine], q_recv.at[h, mine]
+            q_hbm.at[:, q_cols(mine, h)],
+            qbuf.at[unit_of(h, hub), mine],
+            q_recv.at[unit_of(h, hub), mine],
+        )
+
+    def q_up(h, step):
+        other = lax.rem(mine + step, plane_devices)
+        unit = unit_of(h, lax.rem(z, hub + 1))
+        return pltpu.make_async_remote_copy(
+            src_ref=q_hbm.at[:, q_cols(other, h)],
+            dst_ref=qbuf.at[unit, mine],
+            send_sem=q_send.at[h, step],
+            recv_sem=q_recv.at[unit, mine],
+            device_id=at(other, hub),
+            device_id_type=MESH,
         )
 
     def o_copy(h, step):
         other = lax.rem(mine + step, plane_devices)
         return pltpu.make_async_remote_copy(
-            src_ref=obuf.at[h, other],
+            src_ref=obuf.at[unit_of(h, hub), other],
             dst_ref=out_hbm.at[:, q_cols(mine, h)],
-            send_sem=o_send.at[h, step],
+            send_sem=o_send.at[unit_of(h, hub), step],
             recv_sem=o_recv.at[h, mine],
-            device_id={"head": other // sub_size, "sub": other % sub_size},
+            device_id=at(other),
             device_id_type=MESH,
         )
 
     def o_own(h):
         return pltpu.make_async_copy(
-            obuf.at[h, mine], out_hbm.at[:, q_cols(mine, h)], o_recv.at[h, mine]
+            obuf.at[unit_of(h, hub), mine], out_hbm.at[:, q_cols(mine, h)], o_recv.at[h, mine]
+        )
+
+    def o_down(h, r, step):
+        other = lax.rem(mine + step, plane_devices)
+        return pltpu.make_async_remote_copy(
+            src_ref=obuf.at[unit_of(h, r), other],
+            dst_ref=out_hbm.at[:, q_cols(mine, h)],
+            send_sem=o_send.at[unit_of(h, r), step],
+            recv_sem=o_recv.at[h, mine],
+            device_id=at(other, r),
+            device_id_type=MESH,
         )
 
     def kv_source(h, k, p, core):
@@ -284,16 +325,24 @@
             kv_source(h, k, p, s), kvbuf.at[h, k, p], kv_recv.at[h, k, p]
         )
 
+    def uses(h, r, p):
+        if h < moved:
+            return here(r, p)
+        return r >= hub and any(here(i, p) for i in (range(hub + 1) if r == hub else [r]))
+
+    def hands_down(h, r, p):
+        return any(uses(h, i, p) for i in range(r))
+
     def each_source(h, k, remote_act, own_act):
         for p in range(live):
             @pl.when((z == plane_of[p]) & (s == core_of[p]))
             def _():
-                if plane_of[p] > 0 and any(here(r, p) for r in range(plane_of[p])):
+                if hands_down(h, plane_of[p], p):
                     for core in range(sub_size):
                         remote_act(
                             kv_remote(h, k, p, core, core, {"ctx": z - 1, "sub": core})
                         )
-                if here(plane_of[p], p):
+                if uses(h, plane_of[p], p):
                     for step in range(1, sub_size):
                         other = lax.rem(s + step, sub_size)
                         remote_act(
@@ -312,72 +361,136 @@
             device_id_type=MESH,
         )
 
-    takes = [
-        [
-            p
-            for p in range(live)
-            if (plane_of[p] > r and any(here(i, p) for i in range(r + 1))) or here(r, p)
-        ]
-        for r in range(ctx_size)
-    ]
-    passes = [
-        [p for p in range(live) if plane_of[p] > r and any(here(i, p) for i in range(r))]
-        for r in range(ctx_size)
-    ]
-    take_low, take_high = pick([t[0] for t in takes]), pick([t[-1] + 1 for t in takes])
-    pass_low = pick([t[0] if t else 0 for t in passes])
-    pass_high = pick([t[-1] + 1 if t else 0 for t in passes])
-    own_low, own_high = pick(low), pick(high)
-
-    first = jnp.int32(0)
-    for r in range(REQS):
-        first = first + jnp.where(z > r, counts_ref[r], 0)
-    count = jnp.int32(0)
-    for r in range(REQS):
-        count = count + jnp.where(z == r, counts_ref[r], 0)
-    first_pos = first * PAGE
-    query_base = (first + count) * PAGE - QR
+    def bounds(pages):
+        return (
+            pick([t[0] if t else 0 for t in pages]),
+            pick([t[-1] + 1 if t else 0 for t in pages]),
+        )
+
+    def take_bounds(h):
+        return bounds(
+            [
+                [
+                    p
+                    for p in range(live)
+                    if uses(h, r, p) or (plane_of[p] > r and hands_down(h, r, p))
+                ]
+                for r in range(ctx_size)
+            ]
+        )
+
+    def pass_bounds(h):
+        return bounds(
+            [
+                [p for p in range(live) if plane_of[p] > r and hands_down(h, r, p)]
+                for r in range(ctx_size)
+            ]
+        )
+
     token = lax.broadcasted_iota(jnp.int32, (QR, PAGE), 0)
     column = lax.broadcasted_iota(jnp.int32, (QR, PAGE), 1)
     factor = HD ** (-0.5) * math.log2(math.e)
     block = ROW_BLOCK
     heads_in_block = block // QR
 
+    def span_of(r):
+        first, count = jnp.int32(0), jnp.int32(0)
+        for i in range(REQS):
+            first = first + jnp.where(r > i, counts_ref[i], 0)
+            count = count + jnp.where(r == i, counts_ref[i], 0)
+        return first * PAGE, (first + count) * PAGE - QR
+
+    def load_queries(h, unit):
+        for device in range(plane_devices):
+            pltpu.make_async_copy(
+                q_hbm.at[:, q_cols(0, h)], qbuf.at[unit, device], q_recv.at[unit, device]
+            ).wait()
+        for j in range(group):
+            for device in range(plane_devices):
+                qs[pl.ds(j * QR + device * tok_rows, tok_rows), :] = qbuf[
+                    unit, device, :, j * HD : (j + 1) * HD
+                ]
+        mx[...] = jnp.full_like(mx, NEG)
+
+    def close_maxima():
+        for b in range(rows // block):
+            sl = pl.ds(b * block, block)
+            mx[sl, :] = jnp.broadcast_to(jnp.max(mx[sl, :], axis=1, keepdims=True), (block, HD))
+        lsum[...] = jnp.zeros_like(lsum)
+        acc[...] = jnp.zeros_like(acc)
+
+    def score_page(h, p, slot, span):
+        first_pos, query_base = span
+        keys = kvbuf[h, 0, p]
+        pos = p * PAGE + column
+        seen = (pos >= first_pos) & (pos <= query_base + token)
+        bias = jnp.where(seen, 0.0, NEG)
+        for b in range(rows // block):
+            sl = pl.ds(b * block, block)
+            scores = lax.dot_general(
+                qs[sl, :], keys, (((1,), (1,)), ((), ())), preferred_element_type=jnp.float32
+            )
+            scores = scores.reshape(heads_in_block, QR, PAGE) + bias[None]
+            scores = scores.reshape(block, PAGE)
+            sbuf[slot, sl, :] = scores
+            top = mx[sl, :]
+            for c in range(PAGE // HD):
+                top = jnp.maximum(top, scores[:, c * HD : (c + 1) * HD])
+            mx[sl, :] = top
+
+    def value_page(h, p, slot):
+        values = kvbuf[h, 1, p]
+        for b in range(rows // block):
+            sl = pl.ds(b * block, block)
+            top = mx[sl, :]
+            parts = [
+                jnp.exp2((sbuf[slot, sl, c * HD : (c + 1) * HD] - top) * factor)
+                for c in range(PAGE // HD)
+            ]
+            total = lsum[sl, :]
+            for part in parts:
+                total = total + part
+            lsum[sl, :] = total
+            weights = jnp.concatenate([part.astype(jnp.bfloat16) for part in parts], axis=1)
+            acc[sl, :] += jnp.dot(weights, values, preferred_element_type=jnp.float32)
+
+    def finish(unit):
+        for j in range(group):
+            sl = pl.ds(j * QR, QR)
+            done = acc[sl, :] / jnp.sum(lsum[sl, :], axis=1, keepdims=True)
+            done = done.astype(jnp.bfloat16)
+            for device in range(plane_devices):
+                obuf[unit, device, :, j * HD : (j + 1) * HD] = done[
+                    device * tok_rows : (device + 1) * tok_rows, :
+                ]
+
+    def await_page(h, k, p):
+        pltpu.make_async_copy(
+            kv_source(h, k, 0, 0), kvbuf.at[h, k, p], kv_recv.at[h, k, p]
+        ).wait()
+
     def start(copy):
         copy.start()
 
-    order = [(h, k) for h in range(per_core) for k in range(2)]
-    each_source(0, 0, start, start)
-    for h in range(per_core):
+    def own_queries(h):
         for step in range(1, plane_devices):
             q_copy(h, step).start()
         q_own(h).start()
 
-    for turn, (h, k) in enumerate(order):
-        if k == 0:
-            for device in range(plane_devices):
-                pltpu.make_async_copy(
-                    q_hbm.at[:, q_cols(0, h)], qbuf.at[h, device], q_recv.at[h, device]
-                ).wait()
-            for j in range(group):
-                for device in range(plane_devices):
-                    qs[pl.ds(j * QR + device * tok_rows, tok_rows), :] = qbuf[
-                        h, device, :, j * HD : (j + 1) * HD
-                    ]
-            mx[...] = jnp.full_like(mx, NEG)
-        else:
-            for b in range(rows // block):
-                sl = pl.ds(b * block, block)
-                mx[sl, :] = jnp.broadcast_to(
-                    jnp.max(mx[sl, :], axis=1, keepdims=True), (block, HD)
-                )
-            lsum[...] = jnp.zeros_like(lsum)
-            acc[...] = jnp.zeros_like(acc)
-
-        def turn_page(p, carry, h=h, k=k):
-            pltpu.make_async_copy(
-                kv_source(h, k, 0, 0), kvbuf.at[h, k, p], kv_recv.at[h, k, p]
-            ).wait()
+    def own_outputs(h):
+        for step in range(1, plane_devices):
+            o_copy(h, step).start()
+        o_own(h).start()
+
+    own_span = span_of(z)
+    own_low, own_high = pick(low), pick(high)
+
+    def stream(h, k, then=None):
+        take_low, take_high = take_bounds(h)
+        pass_low, pass_high = pass_bounds(h)
+
+        def turn_page(p, carry):
+            await_page(h, k, p)
 
             @pl.when((p >= pass_low) & (p < pass_high))
             def _():
@@ -385,72 +498,129 @@
 
             @pl.when((p >= own_low) & (p < own_high))
             def _():
-                field = kvbuf[h, k, p]
-                slot = p - own_low
                 if k == 0:
-                    pos = p * PAGE + column
-                    seen = (pos >= first_pos) & (pos <= query_base + token)
-                    bias = jnp.where(seen, 0.0, NEG)
-                    for b in range(rows // block):
-                        sl = pl.ds(b * block, block)
-                        scores = lax.dot_general(
-                            qs[sl, :],
-                            field,
-                            (((1,), (1,)), ((), ())),
-                            preferred_element_type=jnp.float32,
-                        )
-                        scores = scores.reshape(heads_in_block, QR, PAGE) + bias[None]
-                        scores = scores.reshape(block, PAGE)
-                        sbuf[slot, sl, :] = scores
-                        top = mx[sl, :]
-                        for c in range(PAGE // HD):
-                            top = jnp.maximum(top, scores[:, c * HD : (c + 1) * HD])
-                        mx[sl, :] = top
+                    score_page(h, p, p - own_low, own_span)
                 else:
-                    for b in range(rows // block):
-                        sl = pl.ds(b * block, block)
-                        top = mx[sl, :]
-                        parts = [
-                            jnp.exp2((sbuf[slot, sl, c * HD : (c + 1) * HD] - top) * factor)
-                            for c in range(PAGE // HD)
-                        ]
-                        total = lsum[sl, :]
-                        for part in parts:
-                            total = total + part
-                        lsum[sl, :] = total
-                        weights = jnp.concatenate(
-                            [part.astype(jnp.bfloat16) for part in parts], axis=1
-                        )
-                        acc[sl, :] += jnp.dot(
-                            weights, field, preferred_element_type=jnp.float32
-                        )
+                    value_page(h, p, p - own_low)
 
             return carry
 
         lax.fori_loop(take_low, take_high, turn_page, 0)
-        if turn + 1 < len(order):
-            each_source(*order[turn + 1], start, start)
+
+    def own_head(h, between=None):
+        load_queries(h, unit_of(h, hub))
+        stream(h, 0)
+        if between is not None:
+            between()
+        close_maxima()
+        stream(h, 1)
+        finish(unit_of(h, hub))
+        own_outputs(h)
+
+    order = [(h, k) for h in range(moved) for k in range(2)]
+    rest = [(h, k) for h in range(moved, per_core) for k in range(2)]
+    each_source(*order[0], start, start)
+    for h in range(moved, per_core):
+        @pl.when(z < hub)
+        def _():
+            for step in range(plane_devices):
+                q_up(h, step).start()
+
+    for h in range(moved):
+        own_queries(h)
+    for h in range(moved, per_core):
+        @pl.when(z >= hub)
+        def _():
+            own_queries(h)
+
+    for h, k in rest:
+        if k == 0:
+            each_source(h, k, start, start)
+
+    @pl.when(z > hub)
+    def _():
+        for h, k in order[1:]:
+            each_source(h, k, start, start)
+
+    for h, k in rest:
         if k == 1:
-            for j in range(group):
-                sl = pl.ds(j * QR, QR)
-                done = acc[sl, :] / jnp.sum(lsum[sl, :], axis=1, keepdims=True)
-                done = done.astype(jnp.bfloat16)
-                for device in range(plane_devices):
-                    obuf[h, device, :, j * HD : (j + 1) * HD] = done[
-                        device * tok_rows : (device + 1) * tok_rows, :
-                    ]
-            for step in range(1, plane_devices):
-                o_copy(h, step).start()
-            o_own(h).start()
+            each_source(h, k, start, start)
+
+    def rest_of_order(turn):
+        if turn < len(order):
+
+            @pl.when(z <= hub)
+            def _():
+                each_source(*order[turn], start, start)
+
+    for h in range(moved):
+        own_head(h, lambda h=h: rest_of_order(2 * h + 1))
+        rest_of_order(2 * h + 2)
+
+    for h in range(moved, per_core):
+        @pl.when(z > hub)
+        def _():
+            own_head(h)
+
+        @pl.when(z == hub)
+        def _():
+            known = min(p for p in range(live) if uses(h, hub, p))
+            for r in range(hub + 1):
+                unit = unit_of(h, r)
+                span = span_of(r)
+                load_queries(h, unit)
+                for k in range(2):
+
+                    def arrive(p, carry, k=k):
+                        await_page(h, k, p)
+                        return carry
+
+                    def turn_page(p, carry, k=k, r=r, span=span):
+                        if k == 0:
+                            score_page(h, p, p - low[r], span)
+                        else:
+                            value_page(h, p, p - low[r])
+                        return carry
+
+                    lax.fori_loop(known, high[r], arrive, 0)
+                    if k == 1:
+                        close_maxima()
+                    lax.fori_loop(low[r], high[r], turn_page, 0)
+                known = high[r]
+                finish(unit)
+                if r < hub:
+                    for step in range(plane_devices):
+                        o_down(h, r, step).start()
+                else:
+                    own_outputs(h)
 
     for h in range(per_core):
         for device in range(plane_devices):
             pltpu.make_async_copy(
-                obuf.at[h, device], out_hbm.at[:, q_cols(0, h)], o_recv.at[h, device]
+                obuf.at[0, device], out_hbm.at[:, q_cols(0, h)], o_recv.at[h, device]
             ).wait()
-        for step in range(1, plane_devices):
-            q_copy(h, step).wait_send()
-            o_copy(h, step).wait_send()
+
+        def drain_own():
+            for step in range(1, plane_devices):
+                q_copy(h, step).wait_send()
+                o_copy(h, step).wait_send()
+
+        if h < moved:
+            drain_own()
+        else:
+            pl.when(z >= hub)(drain_own)
+
+            @pl.when(z < hub)
+            def _():
+                for step in range(plane_devices):
+                    q_up(h, step).wait_send()
+
+            @pl.when(z == hub)
+            def _():
+                for r in range(hub):
+                    for step in range(plane_devices):
+                        o_down(h, r, step).wait_send()
+
         for k in range(2):
             each_source(h, k, lambda copy: copy.wait_send(), None)
 
@@ -458,7 +628,7 @@
                 relay(h, k, p).wait_send()
                 return carry
 
-            lax.fori_loop(pass_low, pass_high, drain, 0)
+            lax.fori_loop(*pass_bounds(h), drain, 0)
 
 
 def shipped(queries, kv_cache, page_counts):
@@ -468,7 +638,8 @@
     pages_here = kv_cache.shape[1] // PAGE
     per_core = local_heads // sub_size
     group = HQ // KVH
-    live, low, high, _, _ = page_plan(ctx_size, sub_size, pages_here)
+    live, low, high, plane_of, _ = page_plan(ctx_size, sub_size, pages_here)
+    units = per_core - per_core // 2 + per_core // 2 * (plane_of[0] + 1)
     slots = max(b - a for a, b in zip(low, high))
     plane_devices = head_size * sub_size
     tok_rows = queries.shape[0]
@@ -485,23 +656,23 @@
         out_specs=pl.BlockSpec(memory_space=pl.ANY),
         scratch_shapes=[
             pltpu.VMEM((per_core, 2, live, PAGE, HD), jnp.bfloat16),
-            pltpu.VMEM((per_core, plane_devices, tok_rows, group * HD), jnp.bfloat16),
+            pltpu.VMEM((units, plane_devices, tok_rows, group * HD), jnp.bfloat16),
             pltpu.VMEM((rows, HD), jnp.bfloat16),
             pltpu.VMEM((slots, rows, PAGE), jnp.float32),
             pltpu.VMEM((rows, HD), jnp.float32),
             pltpu.VMEM((rows, HD), jnp.float32),
             pltpu.VMEM((rows, HD), jnp.float32),
-            pltpu.VMEM((per_core, plane_devices, tok_rows, group * HD), jnp.bfloat16),
+            pltpu.VMEM((units, plane_devices, tok_rows, group * HD), jnp.bfloat16),
             dma((per_core, plane_devices)),
-            dma((per_core, plane_devices)),
-            dma((per_core, plane_devices)),
+            dma((units, plane_devices)),
+            dma((units, plane_devices)),
             dma((per_core, plane_devices)),
             dma((per_core, 2, 2 * sub_size - 1, live)),
             dma((per_core, 2, live)),
             dma((per_core, 2, live)),
         ],
         compiler_params=pltpu.CompilerParams(
-            collective_id=0, has_side_effects=True, vmem_limit_bytes=40 * 1024 * 1024
+            collective_id=0, has_side_effects=True, vmem_limit_bytes=67043328
         ),
     )(page_counts, queries, kv_cache)
 

time: 53.6 us -> 40.4 us (0.75)
  the two profiles are of different devices: /device:TPU:1 before, /device:TPU:11 now
where the time goes in v2:
time: 40.4 us; the launch traced here: 40.1 us
  Pallas kernels  38.3 us (95%)
  local copies, waits for them, and re-layouts  1.87 us (5%)
    pallas_call x1, Pallas kernels, shipped(): pl.pallas_call(functools.partial(ship_kernel, (ctx_size, sub_size, head_s...  38.3 us
    unnamed x1, local copies, waits for them, and re-layouts  1.87 us

profile of v2, /device:TPU:11, one launch (start us, length us, event | category | flops | bytes accessed | tf_op | source)
XLA Modules:
  0.0 40.1 jit_solution(13997836672508858350)
XLA Ops:
  0.0 38.3 %shard_map.37 = bf16[16,16384]{1,0:T(8,128)(2,1)} custom-call(s32[4]{0:T(128)} %counts_ref.1, bf16[16,16384]{1,0:T(8,128)(2,1)} %q_hbm.1, bf16[2,512,512]{2,1,0:T(8,128)(2,1)} %kv_hbm.1), custom_call_target="tpu_custom_call" | custom-call | tf_op jit(solution)/shard_map/pallas_call | solution.py:648
  38.3 1.9 %copy.5 = bf16[16,16384]{1,0:T(8,128)(2,1)} copy(bf16[16,16384]{1,0:T(8,128)(2,1)} %shard_map.37) | data formatting | bytes 1048576

commit v3 on v2

--- a/solution.py
+++ b/solution.py
@@ -533,18 +533,13 @@
         def _():
             own_queries(h)
 
-    for h, k in rest:
-        if k == 0:
-            each_source(h, k, start, start)
-
     @pl.when(z > hub)
     def _():
         for h, k in order[1:]:
             each_source(h, k, start, start)
 
     for h, k in rest:
-        if k == 1:
-            each_source(h, k, start, start)
+        each_source(h, k, start, start)
 
     def rest_of_order(turn):
         if turn < len(order):

time: 40.4 us -> 40.7 us (level)
  the two profiles are of different devices: /device:TPU:11 before, /device:TPU:1 now
where the time goes in v3:
time: 40.7 us; the launch traced here: 40.5 us
  Pallas kernels  38.6 us (95%)
  local copies, waits for them, and re-layouts  1.87 us (5%)
    pallas_call x1, Pallas kernels, shipped(): pl.pallas_call(functools.partial(ship_kernel, (ctx_size, sub_size, head_s...  38.6 us
    unnamed x1, local copies, waits for them, and re-layouts  1.87 us

profile of v3, /device:TPU:1, one launch (start us, length us, event | category | flops | bytes accessed | tf_op | source)
XLA Modules:
  0.0 40.5 jit_solution(7242392279187565546)
XLA Ops:
  0.0 38.6 %shard_map.37 = bf16[16,16384]{1,0:T(8,128)(2,1)} custom-call(s32[4]{0:T(128)} %counts_ref.1, bf16[16,16384]{1,0:T(8,128)(2,1)} %q_hbm.1, bf16[2,512,512]{2,1,0:T(8,128)(2,1)} %kv_hbm.1), custom_call_target="tpu_custom_call" | custom-call | tf_op jit(solution)/shard_map/pallas_call | solution.py:643
  38.6 1.9 %copy.5 = bf16[16,16384]{1,0:T(8,128)(2,1)} copy(bf16[16,16384]{1,0:T(8,128)(2,1)} %shard_map.37) | data formatting | bytes 1048576

commit v4 on v3

--- a/solution.py
+++ b/solution.py
@@ -482,6 +482,16 @@
             o_copy(h, step).start()
         o_own(h).start()
 
+    def drain_pages(h):
+        for k in range(2):
+            each_source(h, k, lambda copy: copy.wait_send(), None)
+
+            def drain(p, carry, k=k):
+                relay(h, k, p).wait_send()
+                return carry
+
+            lax.fori_loop(*pass_bounds(h), drain, 0)
+
     own_span = span_of(z)
     own_low, own_high = pick(low), pick(high)
 
@@ -584,6 +594,9 @@
                 known = high[r]
                 finish(unit)
                 if r < hub:
+                    if r == 0 and h == moved:
+                        for i in range(moved):
+                            drain_pages(i)
                     for step in range(plane_devices):
                         o_down(h, r, step).start()
                 else:
@@ -616,14 +629,14 @@
                     for step in range(plane_devices):
                         o_down(h, r, step).wait_send()
 
-        for k in range(2):
-            each_source(h, k, lambda copy: copy.wait_send(), None)
-
-            def drain(p, carry, h=h, k=k):
-                relay(h, k, p).wait_send()
-                return carry
-
-            lax.fori_loop(*pass_bounds(h), drain, 0)
+        if h < moved and moved < per_core:
+
+            @pl.when(z != hub)
+            def _():
+                drain_pages(h)
+
+        else:
+            drain_pages(h)
 
 
 def shipped(queries, kv_cache, page_counts):

time: 40.7 us -> 40.7 us (level)
  no operation moved by 1% of the time
where the time goes in v4:
time: 40.7 us; the launch traced here: 40.5 us
  Pallas kernels  38.6 us (95%)
  local copies, waits for them, and re-layouts  1.87 us (5%)
    pallas_call x1, Pallas kernels, shipped(): pl.pallas_call(functools.partial(ship_kernel, (ctx_size, sub_size, head_s...  38.6 us
    unnamed x1, local copies, waits for them, and re-layouts  1.87 us

profile of v4, /device:TPU:1, one launch (start us, length us, event | category | flops | bytes accessed | tf_op | source)
XLA Modules:
  0.0 40.5 jit_solution(7082397796988452432)
XLA Ops:
  0.0 38.6 %shard_map.37 = bf16[16,16384]{1,0:T(8,128)(2,1)} custom-call(s32[4]{0:T(128)} %counts_ref.1, bf16[16,16384]{1,0:T(8,128)(2,1)} %q_hbm.1, bf16[2,512,512]{2,1,0:T(8,128)(2,1)} %kv_hbm.1), custom_call_target="tpu_custom_call" | custom-call | tf_op jit(solution)/shard_map/pallas_call | solution.py:656
  38.6 1.9 %copy.5 = bf16[16,16384]{1,0:T(8,128)(2,1)} copy(bf16[16,16384]{1,0:T(8,128)(2,1)} %shard_map.37) | data formatting | bytes 1048576

commit v5 on v4

--- a/solution.py
+++ b/solution.py
@@ -543,24 +543,11 @@
         def _():
             own_queries(h)
 
-    @pl.when(z > hub)
-    def _():
-        for h, k in order[1:]:
-            each_source(h, k, start, start)
-
-    for h, k in rest:
+    for h, k in order[1:] + rest:
         each_source(h, k, start, start)
 
-    def rest_of_order(turn):
-        if turn < len(order):
-
-            @pl.when(z <= hub)
-            def _():
-                each_source(*order[turn], start, start)
-
     for h in range(moved):
-        own_head(h, lambda h=h: rest_of_order(2 * h + 1))
-        rest_of_order(2 * h + 2)
+        own_head(h)
 
     for h in range(moved, per_core):
         @pl.when(z > hub)

time: 40.7 us -> 42.7 us (1.049)
  Pallas kernels: 38.6 us -> 40.6 us
    pallas_call x1, Pallas kernels: 38.6 us -> 40.6 us  [shipped(): pl.pallas_call(functools.partial(ship_kernel, (ctx_size, sub_size, head_s...]
where the time goes in v5:
time: 42.7 us; the launch traced here: 42.5 us
  Pallas kernels  40.6 us (95%)
  local copies, waits for them, and re-layouts  1.87 us (4%)
    pallas_call x1, Pallas kernels, shipped(): pl.pallas_call(functools.partial(ship_kernel, (ctx_size, sub_size, head_s...  40.6 us
    unnamed x1, local copies, waits for them, and re-layouts  1.87 us

profile of v5, /device:TPU:1, one launch (start us, length us, event | category | flops | bytes accessed | tf_op | source)
XLA Modules:
  0.0 42.5 jit_solution(1158989231167517382)
XLA Ops:
  0.0 40.6 %shard_map.37 = bf16[16,16384]{1,0:T(8,128)(2,1)} custom-call(s32[4]{0:T(128)} %counts_ref.1, bf16[16,16384]{1,0:T(8,128)(2,1)} %q_hbm.1, bf16[2,512,512]{2,1,0:T(8,128)(2,1)} %kv_hbm.1), custom_call_target="tpu_custom_call" | custom-call | tf_op jit(solution)/shard_map/pallas_call | solution.py:643
  40.6 1.9 %copy.5 = bf16[16,16384]{1,0:T(8,128)(2,1)} copy(bf16[16,16384]{1,0:T(8,128)(2,1)} %shard_map.37) | data formatting | bytes 1048576
